TPU v7x, 32 devices: a whole 2x2x4 slice. The times are simulated.
32 devices in a mesh: dp: 2 (over core), ctx: 4 (over y, x), tp: 4 (over z).
Axes of the slice: x: 2, y: 2, z: 4, core: 2. Of those that a mesh axis runs over, the one named last changes fastest.
Arguments:
- inputs: bfloat16 [24, 1024, 512], P('dp', 'ctx'), may hold values from -6 to 6
- lengths: int32 [24], P('dp'), may hold values from 256 to 1024, as said below
- norm_gain: float32 [512], P('dp'), may hold values from 0.5 to 1.5
- skip_weight: float32 [512], P('dp'), may hold values from -3 to 3
- lambda_re: float32 [384], P(('tp', 'dp')), may hold values from -1 to -0.1
- lambda_im: float32 [384], P(('tp', 'dp')), may hold values from -20 to 20
- log_step: float32 [384], P(('tp', 'dp')), may hold values from -6.9 to -3
- b_re: bfloat16 [384, 512], P('tp', 'dp'), may hold values from -0.25 to 0.25
- b_im: bfloat16 [384, 512], P('tp', 'dp'), may hold values from -0.25 to 0.25
- c_re: bfloat16 [512, 384], P('dp', 'tp'), may hold values from -0.875 to 0.875
- c_im: bfloat16 [512, 384], P('dp', 'tp'), may hold values from -0.875 to 0.875
- glu_weight: bfloat16 [512, 512], P('dp', 'tp'), may hold values from -0.25 to 0.25
- glu_bias: float32 [512], P(('tp', 'dp')), may hold values from -3 to 3
- out_grad: bfloat16 [24, 1024, 512], P('dp', 'ctx', 'tp'), may hold values from -6 to 6
Outputs:
- output: bfloat16 [24, 1024, 512], P('dp', 'ctx', 'tp')
- input_grad: float32 [24, 1024, 512], P('dp', 'ctx', 'tp')
- grad_norm_gain: float32 [512], P('dp')
- grad_skip: float32 [512], P('dp')
- grad_lambda_re: float32 [384], P(('tp', 'dp'))
- grad_lambda_im: float32 [384], P(('tp', 'dp'))
- grad_log_step: float32 [384], P(('tp', 'dp'))
- grad_b_re: float32 [384, 512], P('tp', 'dp')
- grad_b_im: float32 [384, 512], P('tp', 'dp')
- grad_c_re: float32 [512, 384], P('dp', 'tp')
- grad_c_im: float32 [512, 384], P('dp', 'tp')
- grad_glu_weight: float32 [512, 512], P('dp', 'tp')
- grad_glu_bias: float32 [512], P(('tp', 'dp'))
Inputs may be any that keep to these rules, and one draw needn't show every extreme that they name: `lengths`: each sequence's valid length lies between 256 and 1024; some sequence has exactly 1024.
All inputs are finite; a program needn't handle non-finite values.
Results may differ from a plain program's by a relative error of at most 0.02.
Values may be sent and summed in bfloat16 or wider, within the bound.
A program may use at most 128 MiB of HBM per device.

v0:
```python
import functools

import jax
import jax.numpy as jnp
from jax import lax
from jax.experimental import pallas as pl
from jax.experimental.pallas import tpu as pltpu
from jax.sharding import PartitionSpec as P

epsilon = 1e-05


def carried_in(value, axis, combine, identity, reverse):
    count, index = (lax.axis_size(axis), lax.axis_index(axis))
    everything = jax.tree.map(lambda part: lax.all_gather(part, axis), value)
    start = jax.tree.map(
        lambda part, zero: jnp.broadcast_to(jnp.asarray(zero, part.dtype), part.shape),
        value,
        identity,
    )

    def lap(k, before):
        at = count - 1 - k if reverse else k
        reached = at > index if reverse else at < index
        new = combine(before, jax.tree.map(lambda part: part[at], everything))
        return jax.tree.map(lambda a, b: jnp.where(reached, a, b), new, before)

    return lax.fori_loop(0, count, lap, start)


def contract(left, right, left_dim, right_dim):
    return lax.dot_general(
        left, right, (((left_dim,), (right_dim,)), ((), ())), preferred_element_type=jnp.float32
    )


def combine(earlier, later):
    e_re, e_im, eb_re, eb_im = earlier
    l_re, l_im, lb_re, lb_im = later
    return (
        e_re * l_re - e_im * l_im,
        e_re * l_im + e_im * l_re,
        l_re * eb_re - l_im * eb_im + lb_re,
        l_re * eb_im + l_im * eb_re + lb_im,
    )


def discretize(lam_re, lam_im, step_log, mat_re, mat_im):
    step = jnp.exp(step_log)
    magnitude = jnp.exp(lam_re * step)
    decay_re = magnitude * jnp.cos(lam_im * step)
    decay_im = magnitude * jnp.sin(lam_im * step)
    denom = lam_re * lam_re + lam_im * lam_im
    coef_re = ((decay_re - 1.0) * lam_re + decay_im * lam_im) / denom
    coef_im = (decay_im * lam_re - (decay_re - 1.0) * lam_im) / denom
    bar_re = coef_re[:, None] * mat_re - coef_im[:, None] * mat_im
    bar_im = coef_re[:, None] * mat_im + coef_im[:, None] * mat_re
    return (decay_re, decay_im, jnp.concatenate([bar_re, bar_im], 0))


def normalize(tokens, gain):
    mean_val = jnp.mean(tokens, -1, keepdims=True)
    centered = tokens - mean_val
    var_val = jnp.mean(centered * centered, -1, keepdims=True)
    return centered * lax.rsqrt(var_val + epsilon) * gain


def powers(lam_re, lam_im, step_log, count):
    step = jnp.exp(step_log)
    exponent = (jnp.arange(count, dtype=jnp.float32) + 1.0)[:, None]
    magnitude = jnp.exp(exponent * lam_re * step)
    return (
        magnitude * jnp.cos(exponent * lam_im * step),
        magnitude * jnp.sin(exponent * lam_im * step),
    )


def on_device(
    inputs,
    lengths,
    norm_gain,
    skip_weight,
    lambda_re,
    lambda_im,
    log_step,
    b_re,
    b_im,
    c_re,
    c_im,
    glu_weight,
    glu_bias,
    out_grad,
):
    full_bre, full_bim, full_cre, full_cim, full_glu = (
        lax.all_gather(b_re, "dp", axis=1, tiled=True),
        lax.all_gather(b_im, "dp", axis=1, tiled=True),
        lax.all_gather(c_re, "dp", axis=0, tiled=True),
        lax.all_gather(c_im, "dp", axis=0, tiled=True),
        lax.all_gather(glu_weight, "dp", axis=0, tiled=True),
    )
    gain, skip_full, lam_re, lam_im, step_log, bias_vec = (
        lax.all_gather(norm_gain, "dp", axis=0, tiled=True),
        lax.all_gather(skip_weight, "dp", axis=0, tiled=True),
        lax.all_gather(lambda_re, "dp", axis=0, tiled=True),
        lax.all_gather(lambda_im, "dp", axis=0, tiled=True),
        lax.all_gather(log_step, "dp", axis=0, tiled=True),
        lax.all_gather(glu_bias, "dp", axis=0, tiled=True),
    )
    seq_count, blk_len, feat_dim = inputs.shape
    row_count = seq_count * blk_len
    state_count = full_bre.shape[0]
    unit_count = full_glu.shape[1]
    tp_rank = lax.axis_index("tp")
    unit_start = tp_rank * unit_count
    positions = lax.axis_index("ctx") * blk_len + jnp.arange(blk_len, dtype=jnp.int32)
    valid_mask = (positions[None, :] < lengths[:, None]).astype(jnp.float32).reshape(row_count, 1)
    tokens = inputs.astype(jnp.float32).reshape(row_count, feat_dim)
    tokens_mine = lax.dynamic_slice_in_dim(tokens, unit_start, unit_count, 1)
    cotangent = out_grad.astype(jnp.float32).reshape(row_count, unit_count)
    normed_f, norm_pull = jax.vjp(normalize, tokens, gain)
    normed_b = normed_f.astype(jnp.bfloat16)
    normed_r = normed_b.astype(jnp.float32)
    (decay_re, decay_im, bar_full), disc_pull = jax.vjp(
        discretize,
        lam_re,
        lam_im,
        step_log,
        full_bre.astype(jnp.float32),
        full_bim.astype(jnp.float32),
    )
    bar_b = bar_full.astype(jnp.bfloat16)
    drive = contract(normed_b, bar_b, 1, 1).reshape(seq_count, blk_len, 2 * state_count)
    full_re = jnp.broadcast_to(decay_re, (seq_count, blk_len, state_count))
    full_im = jnp.broadcast_to(decay_im, (seq_count, blk_len, state_count))
    local_states = lax.associative_scan(
        combine, (full_re, full_im, drive[..., :state_count], drive[..., state_count:]), axis=1
    )
    pow_re, pow_im = powers(lam_re, lam_im, step_log, blk_len)
    identity = (
        jnp.ones((1, state_count), jnp.float32),
        jnp.zeros((1, state_count), jnp.float32),
        jnp.zeros((seq_count, state_count), jnp.float32),
        jnp.zeros((seq_count, state_count), jnp.float32),
    )
    incoming = carried_in(
        (pow_re[-1:], pow_im[-1:], local_states[2][:, -1], local_states[3][:, -1]),
        "ctx",
        combine,
        identity,
        False,
    )
    in_re = incoming[2][:, None, :]
    in_im = incoming[3][:, None, :]
    state_re = local_states[2] + pow_re * in_re - pow_im * in_im
    state_im = local_states[3] + pow_re * in_im + pow_im * in_re
    states_b = (
        jnp.concatenate([state_re, state_im], -1)
        .reshape(row_count, 2 * state_count)
        .astype(jnp.bfloat16)
    )
    c_stack = jnp.concatenate([full_cre, -full_cim], 1)
    ssm_part = contract(states_b, c_stack, 1, 1)
    ssm_full = lax.psum(ssm_part.astype(jnp.bfloat16), "tp").astype(jnp.float32)
    pre_full = ssm_full + skip_full * normed_r
    gelu_full, gelu_pull = jax.vjp(jax.nn.gelu, pre_full)
    gelu_b = gelu_full.astype(jnp.bfloat16)
    gelu_part = lax.dynamic_slice_in_dim(gelu_b, unit_start, unit_count, 1)
    gelu_mine = gelu_part.astype(jnp.float32)
    gate = contract(gelu_b, full_glu, 1, 0) + bias_vec
    gate_sig = jax.nn.sigmoid(gate)
    output = (
        (valid_mask * (tokens_mine + gelu_mine * gate_sig))
        .astype(jnp.bfloat16)
        .reshape(seq_count, blk_len, unit_count)
    )
    branch_grad = valid_mask * cotangent
    gate_grad = branch_grad * gelu_mine * gate_sig * (1.0 - gate_sig)
    bias_grad = jnp.sum(gate_grad, 0)
    gate_b = gate_grad.astype(jnp.bfloat16)
    glu_grad = contract(gelu_b, gate_b, 0, 0)
    gelu_grad = contract(gate_b, full_glu, 1, 1)
    own_cols = (
        lax.dynamic_slice_in_dim(gelu_grad, unit_start, unit_count, 1) + branch_grad * gate_sig
    )
    gelu_grad = lax.dynamic_update_slice_in_dim(gelu_grad, own_cols, unit_start, 1)
    gelu_back = lax.psum(gelu_grad, "tp")
    (pre_grad,) = gelu_pull(gelu_back)
    skip_grad = jnp.sum(pre_grad * normed_r, 0)
    pre_b = pre_grad.astype(jnp.bfloat16)
    state_grad = contract(pre_b, c_stack, 1, 0).reshape(seq_count, blk_len, 2 * state_count)
    c_grad = contract(pre_b, states_b, 0, 0)
    back_local = lax.associative_scan(
        combine,
        (full_re, -full_im, state_grad[..., :state_count], state_grad[..., state_count:]),
        axis=1,
        reverse=True,
    )
    later_adj = carried_in(
        (pow_re[-1:], -pow_im[-1:], back_local[2][:, 0], back_local[3][:, 0]),
        "ctx",
        combine,
        identity,
        True,
    )
    rev_re = pow_re[::-1]
    rev_im = -pow_im[::-1]
    next_re = later_adj[2][:, None, :]
    next_im = later_adj[3][:, None, :]
    adj_re = back_local[2] + rev_re * next_re - rev_im * next_im
    adj_im = back_local[3] + rev_re * next_im + rev_im * next_re
    prev_re = jnp.concatenate([in_re, state_re[:, :-1]], 1)
    prev_im = jnp.concatenate([in_im, state_im[:, :-1]], 1)
    decay_grad_re = jnp.sum(adj_re * prev_re + adj_im * prev_im, (0, 1))
    decay_grad_im = jnp.sum(adj_im * prev_re - adj_re * prev_im, (0, 1))
    adj_b = (
        jnp.concatenate([adj_re, adj_im], -1)
        .reshape(row_count, 2 * state_count)
        .astype(jnp.bfloat16)
    )
    bar_grad = contract(adj_b, normed_b, 0, 0)
    normed_part = contract(adj_b, bar_b, 1, 0)
    normed_sum = lax.psum(normed_part.astype(jnp.bfloat16), "tp").astype(jnp.float32)
    normed_grad = normed_sum + skip_full * pre_grad
    token_grad, gain_grad = norm_pull(normed_grad)
    input_grad = (
        valid_mask * cotangent + lax.dynamic_slice_in_dim(token_grad, unit_start, unit_count, 1)
    ).reshape(seq_count, blk_len, unit_count)
    grad_cre = c_grad[:, :state_count]
    grad_cim = -c_grad[:, state_count:]
    lre_grad, lim_grad, step_grad, bre_grad, bim_grad = disc_pull(
        (decay_grad_re, decay_grad_im, bar_grad)
    )
    shards = (
        lax.psum_scatter(
            gain_grad.astype(jnp.bfloat16), "dp", scatter_dimension=0, tiled=True
        ).astype(jnp.float32),
        lax.psum_scatter(
            skip_grad.astype(jnp.bfloat16), "dp", scatter_dimension=0, tiled=True
        ).astype(jnp.float32),
        lax.psum_scatter(
            lre_grad.astype(jnp.bfloat16), "dp", scatter_dimension=0, tiled=True
        ).astype(jnp.float32),
        lax.psum_scatter(
            lim_grad.astype(jnp.bfloat16), "dp", scatter_dimension=0, tiled=True
        ).astype(jnp.float32),
        lax.psum_scatter(
            step_grad.astype(jnp.bfloat16), "dp", scatter_dimension=0, tiled=True
        ).astype(jnp.float32),
        lax.psum_scatter(
            bias_grad.astype(jnp.bfloat16), "dp", scatter_dimension=0, tiled=True
        ).astype(jnp.float32),
        lax.psum_scatter(
            bre_grad.astype(jnp.bfloat16), "dp", scatter_dimension=1, tiled=True
        ).astype(jnp.float32),
        lax.psum_scatter(
            bim_grad.astype(jnp.bfloat16), "dp", scatter_dimension=1, tiled=True
        ).astype(jnp.float32),
        lax.psum_scatter(
            grad_cre.astype(jnp.bfloat16), "dp", scatter_dimension=0, tiled=True
        ).astype(jnp.float32),
        lax.psum_scatter(
            grad_cim.astype(jnp.bfloat16), "dp", scatter_dimension=0, tiled=True
        ).astype(jnp.float32),
        lax.psum_scatter(
            glu_grad.astype(jnp.bfloat16), "dp", scatter_dimension=0, tiled=True
        ).astype(jnp.float32),
    )
    summed = (
        lax.psum(shards[0].astype(jnp.bfloat16), "ctx").astype(jnp.float32),
        lax.psum(shards[1].astype(jnp.bfloat16), "ctx").astype(jnp.float32),
        lax.psum(shards[2].astype(jnp.bfloat16), "ctx").astype(jnp.float32),
        lax.psum(shards[3].astype(jnp.bfloat16), "ctx").astype(jnp.float32),
        lax.psum(shards[4].astype(jnp.bfloat16), "ctx").astype(jnp.float32),
        lax.psum(shards[5].astype(jnp.bfloat16), "ctx").astype(jnp.float32),
        lax.psum(shards[6].astype(jnp.bfloat16), "ctx").astype(jnp.float32),
        lax.psum(shards[7].astype(jnp.bfloat16), "ctx").astype(jnp.float32),
        lax.psum(shards[8].astype(jnp.bfloat16), "ctx").astype(jnp.float32),
        lax.psum(shards[9].astype(jnp.bfloat16), "ctx").astype(jnp.float32),
        lax.psum(shards[10].astype(jnp.bfloat16), "ctx").astype(jnp.float32),
    )
    return (
        output,
        input_grad,
        summed[0],
        summed[1],
        summed[2],
        summed[3],
        summed[4],
        summed[6],
        summed[7],
        summed[8],
        summed[9],
        summed[10],
        summed[5],
    )


MESH = pl.DeviceIdType.MESH
SQ2PI = 0.7978845608028654


def nt(a, b):
    return lax.dot_general(a, b, (((1,), (1,)), ((), ())), preferred_element_type=jnp.float32)


def nn(a, b):
    return lax.dot_general(a, b, (((1,), (0,)), ((), ())), preferred_element_type=jnp.float32)


def tn(a, b):
    return lax.dot_general(a, b, (((0,), (0,)), ((), ())), preferred_element_type=jnp.float32)


def cmul(ar, ai, br, bi):
    return ar * br - ai * bi, ar * bi + ai * br


def lane(start, size):
    return pl.ds(pl.multiple_of(start, 128), size)


def fused_body(geo, *refs):
    D, C, T, S, L, H, N, U = geo
    R = S * L
    NS = N // T
    HD = H // D
    f32, bf16 = jnp.float32, jnp.bfloat16
    (len_ref, x_hbm, og_hbm, pk1, pk2, sm_ref, out_hbm, tg_hbm, fc_ref, fg_ref, fb_ref, fv_ref) = refs[:12]
    (xv, nrm, xh, rs, raw, st, sb, tmp, act, gp, sig, ogv, ob, gl, pg, plb, mu, nb, tgb,
     w4, gt, smr, cst, ce, cer, cbr, gc, gg, gb, r1c, r1g, r1b, s1c, s1g, s1b, r2c, r2g, r2b,
     s2c, s2g, s2b, r3c, r3g, r3b, vv, vr1, vr2, vr3, lsem, ssem, rsem) = refs[12:]
    d, c, t = lax.axis_index("dp"), lax.axis_index("ctx"), lax.axis_index("tp")
    zpeer = [(d, c, lax.rem(t + k, T)) for k in range(1, T)]
    cpeer = [(d, lax.rem(c + k, C), t) for k in range(1, C)]
    sib = (1 - d, c, t)
    xpeer = [(1 - d, c, lax.rem(t + k, T)) for k in range(1, T)]
    everyone = zpeer + cpeer + [sib] + xpeer

    count = [0]
    started = []

    def remote(src, dst, peer):
        i = count[0]
        count[0] += 1
        cp = pltpu.make_async_remote_copy(
            src_ref=src, dst_ref=dst, send_sem=ssem.at[i], recv_sem=rsem.at[i],
            device_id=peer, device_id_type=MESH)
        cp.start()
        started.append(cp)
        return cp

    cx = pltpu.make_async_copy(x_hbm.at[pl.ds(pl.multiple_of(R * t, R), R)], xv, lsem.at[0])
    cx.start()
    co = pltpu.make_async_copy(
        og_hbm.at[pl.ds(pl.multiple_of(R * t, R), R)], ogv.at[:, lane(U * t, U)], lsem.at[1])
    co.start()
    barrier = pltpu.get_barrier_semaphore()
    for p in everyone:
        pl.semaphore_signal(barrier, inc=1, device_id=p, device_id_type=MESH)
    pl.semaphore_wait(barrier, len(everyone))

    me8 = d * T + t
    small = [remote(sm_ref, smr.at[me8], p) for p in zpeer + [sib] + xpeer]
    gq, hq = c // 2, lax.rem(c, 2)
    wl = lane(HD * d + 128 * hq, 128)
    w1b = [remote(pk1.at[gq, :, lane(128 * hq, 128)], w4.at[gq, t, :, wl], p) for p in zpeer]
    w1c = [remote(pk1.at[2 + gq, :, lane(128 * hq, 128)], w4.at[2 + gq, t, :, wl], p) for p in zpeer]
    uq = U // C
    grow = pl.ds(pl.multiple_of(uq * c, uq), uq)
    dl = lane(HD * d, HD)
    w1g = [remote(pk2.at[grow], gt.at[t, grow, dl], p) for p in zpeer]
    w4[gq, t, :, wl] = pk1[gq, :, lane(128 * hq, 128)]
    w4[2 + gq, t, :, wl] = pk1[2 + gq, :, lane(128 * hq, 128)]
    gt[t, grow, dl] = pk2[grow]
    smr[me8] = sm_ref[...]

    cx.wait()

    def ln_tile(i, _):
        rows = pl.ds(pl.multiple_of(i * 32, 32), 32)
        x = xv[rows, :].astype(f32)
        cen = x - jnp.mean(x, -1, keepdims=True)
        rstd = lax.rsqrt(jnp.mean(cen * cen, -1, keepdims=True) + epsilon)
        xh[rows, :] = cen * rstd
        rs[rows, :] = jnp.broadcast_to(rstd, (32, 128))
        return 0

    lax.fori_loop(0, R // 32, ln_tile, 0)

    for cp in small:
        cp.wait_recv()
    zero = jnp.zeros((8, H - HD), f32)
    vec = jnp.zeros((8, H), f32)
    bias = jnp.zeros((8, H), f32)
    for dd in range(D):
        for tt in range(T):
            ext = jnp.concatenate([smr[dd * T + tt], zero], 1)
            place = tt * D + dd
            vec = vec + (pltpu.roll(ext, place * (NS // D), 1) if place else ext)
            bias = bias + (pltpu.roll(ext, place * (U // D), 1) if place else ext)
    both = jnp.concatenate([smr[t], smr[T + t]], 1)
    row8 = lax.broadcasted_iota(jnp.int32, (8, N), 0)
    full = lambda v, k, n: jnp.broadcast_to(v[k:k + 1, :n], (8, n))
    dr, di = full(vec, 0, N), full(vec, 1, N)
    cr, ci = full(vec, 2, N), full(vec, 3, N)
    pows = {1: (dr, di)}
    for k in range(2, 9):
        pows[k] = cmul(*pows[k - 1], dr, di)
    for n_, k in ((0, 1), (1, 2), (2, 4)):
        keep = row8 >= k
        cst[2 * n_] = jnp.where(keep, pows[k][0], 0.0)
        cst[2 * n_ + 1] = jnp.where(keep, pows[k][1], 0.0)
        keep = row8 < 8 - k
        cst[8 + 2 * n_] = jnp.where(keep, pows[k][0], 0.0)
        cst[8 + 2 * n_ + 1] = jnp.where(keep, -pows[k][1], 0.0)
    pr, pi, qr, qi = pows[1][0], pows[1][1], pows[8][0], -pows[8][1]
    for r in range(1, 8):
        pr = jnp.where(row8 == r, pows[r + 1][0], pr)
        pi = jnp.where(row8 == r, pows[r + 1][1], pi)
        qr = jnp.where(row8 == r, pows[8 - r][0], qr)
        qi = jnp.where(row8 == r, -pows[8 - r][1], qi)
    cst[6], cst[7], cst[14], cst[15] = pr, pi, qr, qi
    cst[16], cst[17] = pows[8]
    cst[18], cst[19] = cr, ci
    big = pows[8]
    n_ = 8
    while n_ < L:
        big = cmul(*big, *big)
        n_ *= 2
    cst[20], cst[21] = big
    gain_r, skip_r, bias_r = both[5:6, :], both[6:7, :], bias[4:5, :]

    def nrm_tile(i, _):
        rows = pl.ds(pl.multiple_of(i * 32, 32), 32)
        nrm[rows, :] = (xh[rows, :] * gain_r).astype(bf16)
        return 0

    lax.fori_loop(0, R // 32, nrm_tile, 0)

    for cp in w1b:
        cp.wait_recv()
    w2b = [remote(w4.at[gq, :, :, wl], w4.at[gq, :, :, wl], p) for p in cpeer]
    for cp in w1c:
        cp.wait_recv()
    w2c = [remote(w4.at[2 + gq, :, :, wl], w4.at[2 + gq, :, :, wl], p) for p in cpeer]
    for cp in w1g:
        cp.wait_recv()
    w2g = [remote(gt.at[:, grow, dl], gt.at[:, grow, dl], p) for p in cpeer]
    og = [remote(og_hbm.at[pl.ds(pl.multiple_of(R * p[2], R), R)], ogv.at[:, lane(U * t, U)], p)
          for p in zpeer]
    for cp in w2b:
        cp.wait_recv()
    w3b = remote(w4.at[0:2, :, :, dl], w4.at[0:2, :, :, dl], sib)
    for cp in w2c:
        cp.wait_recv()
    w3c = remote(w4.at[2:4, :, :, dl], w4.at[2:4, :, :, dl], sib)
    for cp in w2g:
        cp.wait_recv()
    w3g = remote(gt.at[:, :, dl], gt.at[:, :, dl], sib)

    w3b.wait_recv()

    def seq_rows(s):
        return pl.ds(pl.multiple_of(s * L, L), L)

    def drive_seq(s, _):
        raw[seq_rows(s), :] = nt(nrm[seq_rows(s), :], w4[0:2].reshape(2 * N, H))
        return 0

    lax.fori_loop(0, S, drive_seq, 0)

    def scan_lanes(src, dst, base, coef, reverse, end_ref):
        def lanes_step(j, _):
            lr_, li_ = lane(128 * j, 128), lane(N + 128 * j, 128)
            con = [cst[base + k, :, lr_] for k in range(8)]
            cfr, cfi = cst[18, :, lr_], cst[19, :, lr_]

            def tile(i, carry):
                ii = L // 8 - 1 - i if reverse else i
                out = []
                for s in range(S):
                    rows = pl.ds(pl.multiple_of(s * L + ii * 8, 8), 8)
                    ar, ai = src[rows, lr_], src[rows, li_]
                    if coef:
                        ar, ai = cmul(cfr, cfi, ar, ai)
                    for n_, k in ((0, 1), (1, 2), (2, 4)):
                        sh = 8 - k if reverse else k
                        br, bi = pltpu.roll(ar, sh, 0), pltpu.roll(ai, sh, 0)
                        mr, mi = con[2 * n_], con[2 * n_ + 1]
                        ar, ai = ar + mr * br - mi * bi, ai + mr * bi + mi * br
                    kr, ki = carry[2 * s], carry[2 * s + 1]
                    ar, ai = ar + con[6] * kr - con[7] * ki, ai + con[6] * ki + con[7] * kr
                    dst[rows, lr_] = ar
                    dst[rows, li_] = ai
                    e = 0 if reverse else 7
                    out.append(jnp.broadcast_to(ar[e:e + 1, :], (8, 128)))
                    out.append(jnp.broadcast_to(ai[e:e + 1, :], (8, 128)))
                return tuple(out)

            z = jnp.zeros((8, 128), f32)
            fin = lax.fori_loop(0, L // 8, tile, (z,) * (2 * S))
            for s in range(S):
                end_ref[pl.ds(s, 1), lr_] = fin[2 * s][0:1, :]
                end_ref[pl.ds(S + s, 1), lr_] = fin[2 * s + 1][0:1, :]
            return 0

        lax.fori_loop(0, N // 128, lanes_step, 0)

    scan_lanes(raw, st, 0, True, False, ce.at[0])
    fce = [remote(ce.at[0], cer.at[k], p) for k, p in enumerate(cpeer)]
    for cp in fce:
        cp.wait_recv()

    def incoming(buf, forward):
        bg = (cst[20, 0:1, :], cst[21, 0:1, :])
        wt = (jnp.ones((1, N), f32), jnp.zeros((1, N), f32))
        accr = jnp.zeros((S, N), f32)
        acci = jnp.zeros((S, N), f32)
        for k in range(1, C):
            got = buf[k - 1] if forward else buf[C - 1 - k]
            has = (c >= k) if forward else (c + k < C)
            w = jnp.where(has, 1.0, 0.0)
            vr, vi = got[0:S, :], got[S:2 * S, :]
            wi = wt[1] if forward else -wt[1]
            ur, ui = cmul(wt[0], wi, vr, vi)
            accr = accr + w * ur
            acci = acci + w * ui
            wt = cmul(*wt, *bg)
        return accr, acci

    inr, ini = incoming(cer, True)
    ce[2, 0:S, :] = inr
    ce[2, S:2 * S, :] = ini

    def fix_lanes(j, _):
        lr_, li_ = lane(128 * j, 128), lane(N + 128 * j, 128)
        p0, p1 = cst[6, :, lr_], cst[7, :, lr_]
        e0, e1 = cst[16, :, lr_], cst[17, :, lr_]
        q0 = tuple(jnp.broadcast_to(ce[2, pl.ds(k * S + s, 1), lr_], (8, 128))
                   for s in range(S) for k in range(2))

        def tile(i, q):
            q = list(q)
            for s in range(S):
                rr, ri = [], []
                for h in range(2):
                    rows = pl.ds(pl.multiple_of(s * L + i * 16 + 8 * h, 8), 8)
                    vr, vi = cmul(p0, p1, q[2 * s], q[2 * s + 1])
                    ar, ai = st[rows, lr_] + vr, st[rows, li_] + vi
                    st[rows, lr_] = ar
                    st[rows, li_] = ai
                    rr.append(ar)
                    ri.append(ai)
                    q[2 * s], q[2 * s + 1] = cmul(q[2 * s], q[2 * s + 1], e0, e1)
                rows = pl.ds(pl.multiple_of(s * L + i * 16, 16), 16)
                sb[rows, lr_] = jnp.concatenate(rr, 0).astype(bf16)
                sb[rows, li_] = jnp.concatenate(ri, 0).astype(bf16)
            return tuple(q)

        lax.fori_loop(0, L // 16, tile, q0)
        return 0

    lax.fori_loop(0, N // 128, fix_lanes, 0)

    w3c.wait_recv()

    def ssm_seq(s, _):
        tmp[seq_rows(s), :] = nn(sb[seq_rows(s), :], w4[2:4].reshape(2 * N, H))
        return 0

    lax.fori_loop(0, S, ssm_seq, 0)

    def gelu_tile(i, _):
        rows = pl.ds(pl.multiple_of(i * 32, 32), 32)
        pre = tmp[rows, :] + skip_r * nrm[rows, :].astype(f32)
        sq = pre * pre
        th = jnp.tanh(pre * (SQ2PI + (SQ2PI * 0.044715) * sq))
        half = 0.5 + 0.5 * th
        act[rows, :] = (pre * half).astype(bf16)
        gp[rows, :] = half + 0.5 * pre * (1.0 - th * th) * (SQ2PI + (3 * 0.044715 * SQ2PI) * sq)
        return 0

    lax.fori_loop(0, R // 32, gelu_tile, 0)
    w3g.wait_recv()

    def gate_seq(s, _):
        tmp[seq_rows(s), :] = nt(act[seq_rows(s), :], gt[...].reshape(H, H))
        return 0

    lax.fori_loop(0, S, gate_seq, 0)

    def valid_of(i):
        s = i // (L // 32)
        pos = c * L + lax.rem(i, L // 32) * 32 + lax.broadcasted_iota(jnp.int32, (32, 1), 0)
        return jnp.where(pos < len_ref[S * t + s], 1.0, 0.0)

    def out_tile(i, _):
        rows = pl.ds(pl.multiple_of(i * 32, 32), 32)
        sg = 0.5 + 0.5 * jnp.tanh(0.5 * (tmp[rows, :] + bias_r))
        sig[rows, :] = sg
        o = valid_of(i) * (xv[rows, :].astype(f32) + act[rows, :].astype(f32) * sg)
        ob[rows, :] = o.astype(bf16)
        return 0

    lax.fori_loop(0, R // 32, out_tile, 0)
    mine = pl.ds(pl.multiple_of(R * t, R), R)
    outc = [remote(ob.at[:, lane(U * p[2], U)], out_hbm.at[mine, :], p) for p in zpeer]
    oc = pltpu.make_async_copy(ob.at[:, lane(U * t, U)], out_hbm.at[mine, :], lsem.at[2])
    oc.start()

    co.wait()
    for cp in og:
        cp.wait_recv()

    def fold(v):
        return jnp.sum(v.reshape(4, 8, v.shape[-1]), 0)

    def gate_tile(i, acc):
        rows = pl.ds(pl.multiple_of(i * 32, 32), 32)
        sg = sig[rows, :]
        direct = valid_of(i) * ogv[rows, :].astype(f32) * sg
        gg_ = direct * act[rows, :].astype(f32) * (1.0 - sg)
        gl[rows, :] = gg_.astype(bf16)
        sig[rows, :] = direct
        return acc + fold(gg_)

    bias_g = lax.fori_loop(0, R // 32, gate_tile, jnp.zeros((8, H), f32))

    def actg_seq(s, _):
        tmp[seq_rows(s), :] = nn(gl[seq_rows(s), :], gt[...].reshape(H, H))
        return 0

    lax.fori_loop(0, S, actg_seq, 0)

    def pre_tile(i, acc):
        rows = pl.ds(pl.multiple_of(i * 32, 32), 32)
        p = (tmp[rows, :] + sig[rows, :]) * gp[rows, :]
        pg[rows, :] = p
        plb[rows, :] = p.astype(bf16)
        return acc + fold(p * nrm[rows, :].astype(f32))

    skip_g = lax.fori_loop(0, R // 32, pre_tile, jnp.zeros((8, H), f32))

    def sgrad_seq(s, _):
        mu[seq_rows(s), :] = nt(plb[seq_rows(s), :], w4[2:4].reshape(2 * N, H))
        return 0

    lax.fori_loop(0, S, sgrad_seq, 0)
    scan_lanes(mu, mu, 8, False, True, ce.at[1])
    bce = [remote(ce.at[1], cbr.at[k], p) for k, p in enumerate(cpeer)]

    gcf, gbf, ggf = gc.reshape(2 * N, H), gb.reshape(2 * N, H), gg.reshape(H, H)

    def gc_step(j, _):
        gcf[pl.ds(pl.multiple_of(j * 128, 128), 128), :] = tn(sb[:, lane(j * 128, 128)], plb[...]).astype(bf16)
        return 0

    lax.fori_loop(0, 2 * N // 128, gc_step, 0)
    ol = lane(HD * (1 - d), HD)
    d1c = remote(gc.at[:, :, :, ol], r1c, sib)

    def gg_step(j, _):
        ggf[pl.ds(pl.multiple_of(j * 128, 128), 128), :] = tn(gl[:, lane(j * 128, 128)], act[...]).astype(bf16)
        return 0

    lax.fori_loop(0, H // 128, gg_step, 0)
    d1g = remote(gg.at[:, :, ol], r1g, sib)

    for cp in bce:
        cp.wait_recv()
    inr, ini = incoming(cbr, False)
    ce[2, 0:S, :] = inr
    ce[2, S:2 * S, :] = ini
    row1 = lax.broadcasted_iota(jnp.int32, (8, 128), 0)

    def adj_lanes(j, _):
        lr_, li_ = lane(128 * j, 128), lane(N + 128 * j, 128)
        p0, p1 = cst[14, :, lr_], cst[15, :, lr_]
        e0, e1 = cst[16, :, lr_], -cst[17, :, lr_]
        cfr, cfi = cst[18, :, lr_], cst[19, :, lr_]
        q0 = tuple(jnp.broadcast_to(ce[2, pl.ds(k * S + s, 1), lr_], (8, 128))
                   for s in range(S) for k in range(2))
        z = jnp.zeros((8, 128), f32)

        def tile(i, carry):
            q, m, acc = list(carry[:2 * S]), list(carry[2 * S:4 * S]), list(carry[4 * S:])
            ii = L // 16 - 1 - i
            for s in range(S):
                rr, ri = [None, None], [None, None]
                for h in (1, 0):
                    rows = pl.ds(pl.multiple_of(s * L + ii * 16 + 8 * h, 8), 8)
                    vr, vi = cmul(p0, p1, q[2 * s], q[2 * s + 1])
                    ar, ai = mu[rows, lr_] + vr, mu[rows, li_] + vi
                    q[2 * s], q[2 * s + 1] = cmul(q[2 * s], q[2 * s + 1], e0, e1)
                    nr = jnp.where(row1 == 7, m[2 * s], pltpu.roll(ar, 7, 0))
                    ni = jnp.where(row1 == 7, m[2 * s + 1], pltpu.roll(ai, 7, 0))
                    m[2 * s] = jnp.broadcast_to(ar[0:1, :], (8, 128))
                    m[2 * s + 1] = jnp.broadcast_to(ai[0:1, :], (8, 128))
                    xr, xi = st[rows, lr_], st[rows, li_]
                    acc[0] = acc[0] + nr * xr + ni * xi
                    acc[1] = acc[1] + ni * xr - nr * xi
                    ur, ui = raw[rows, lr_], raw[rows, li_]
                    acc[2] = acc[2] + ar * ur + ai * ui
                    acc[3] = acc[3] + ai * ur - ar * ui
                    rr[h] = cfr * ar + cfi * ai
                    ri[h] = cfr * ai - cfi * ar
                rows = pl.ds(pl.multiple_of(s * L + ii * 16, 16), 16)
                nb[rows, lr_] = jnp.concatenate(rr, 0).astype(bf16)
                nb[rows, li_] = jnp.concatenate(ri, 0).astype(bf16)
            return tuple(q) + tuple(m) + tuple(acc)

        fin = lax.fori_loop(0, L // 16, tile, q0 + q0 + (z,) * 4)
        for k in range(4):
            vv[3 + k:4 + k, lr_] = jnp.sum(fin[4 * S + k], 0, keepdims=True)
        return 0

    vv[...] = jnp.zeros_like(vv)
    lax.fori_loop(0, N // 128, adj_lanes, 0)

    def gb_step(j, _):
        gbf[pl.ds(pl.multiple_of(j * 128, 128), 128), :] = tn(nb[:, lane(j * 128, 128)], nrm[...]).astype(bf16)
        return 0

    lax.fori_loop(0, 2 * N // 128, gb_step, 0)
    d1b = remote(gb.at[:, :, :, ol], r1b, sib)

    def rs_ctx(p):
        return p // 2, pl.ds(pl.multiple_of((NS // 2) * lax.rem(p, 2), NS // 2), NS // 2)

    d1c.wait_recv()
    s1c[...] = (gc[:, :, :, dl].astype(f32) + r1c[...].astype(f32)).astype(bf16)
    d2c = [remote(s1c.at[rs_ctx(p[1])[0], :, rs_ctx(p[1])[1], :], r2c.at[k], p) for k, p in enumerate(cpeer)]
    d1g.wait_recv()
    s1g[...] = (gg[:, :, dl].astype(f32) + r1g[...].astype(f32)).astype(bf16)
    gr = lambda p: pl.ds(pl.multiple_of(uq * p, uq), uq)
    d2g = [remote(s1g.at[:, gr(p[1]), :], r2g.at[k], p) for k, p in enumerate(cpeer)]

    def ng_seq(s, _):
        tmp[seq_rows(s), :] = nn(nb[seq_rows(s), :], w4[0:2].reshape(2 * N, H))
        return 0

    lax.fori_loop(0, S, ng_seq, 0)

    def tok_tile(i, acc):
        rows = pl.ds(pl.multiple_of(i * 32, 32), 32)
        n = tmp[rows, :] + skip_r * pg[rows, :]
        xt = xh[rows, :]
        h = n * gain_r
        m1 = jnp.mean(h, -1, keepdims=True)
        m2 = jnp.mean(h * xt, -1, keepdims=True)
        tgb[rows, :] = ((h - m1 - xt * m2) * rs[rows, 0:1]).astype(bf16)
        return acc + fold(n * xt)

    gain_g = lax.fori_loop(0, R // 32, tok_tile, jnp.zeros((8, H), f32))
    tgc = [remote(tgb.at[:, lane(U * p[2], U)], tg_hbm.at[mine, :], p) for p in zpeer]
    tc = pltpu.make_async_copy(tgb.at[:, lane(U * t, U)], tg_hbm.at[mine, :], lsem.at[3])
    tc.start()
    vv[0:1, :] = jnp.sum(gain_g, 0, keepdims=True)
    vv[1:2, :] = jnp.sum(skip_g, 0, keepdims=True)
    vv[2:3, :] = jnp.sum(bias_g, 0, keepdims=True)

    d1v = remote(vv, vr1, sib)
    d1b.wait_recv()
    s1b[...] = (gb[:, :, :, dl].astype(f32) + r1b[...].astype(f32)).astype(bf16)
    d2b = [remote(s1b.at[rs_ctx(p[1])[0], :, rs_ctx(p[1])[1], :], r2b.at[k], p) for k, p in enumerate(cpeer)]
    d1v.wait_recv()
    vr2[0] = vv[...] + vr1[...]
    d2v = [remote(vr2.at[0], vr2.at[k + 1], p) for k, p in enumerate(cpeer)]

    def total(first, buf, n):
        acc = first.astype(f32)
        for k in range(n):
            acc = acc + buf[k].astype(f32)
        return acc

    for cp in d2c:
        cp.wait_recv()
    s2c[...] = total(s1c[rs_ctx(c)[0], :, rs_ctx(c)[1], :], r2c, C - 1).astype(bf16)
    d3c = [remote(s2c.at[p[2]], r3c.at[k], p) for k, p in enumerate(zpeer)]
    for cp in d2g:
        cp.wait_recv()
    s2g[...] = total(s1g[:, gr(c), :], r2g, C - 1).astype(bf16)
    d3g = [remote(s2g.at[p[2]], r3g.at[k], p) for k, p in enumerate(zpeer)]
    for cp in d2b:
        cp.wait_recv()
    s2b[...] = total(s1b[rs_ctx(c)[0], :, rs_ctx(c)[1], :], r2b, C - 1).astype(bf16)
    d3b = [remote(s2b.at[p[2]], r3b.at[k], p) for k, p in enumerate(zpeer)]
    for cp in d2v:
        cp.wait_recv()
    vr3[0] = vr2[0] + vr2[1] + vr2[2] + vr2[3]
    d3v = [remote(vr3.at[0], vr3.at[k + 1], p) for k, p in enumerate(zpeer)]

    for cp in d3c:
        cp.wait_recv()
    fc_ref[c] = total(s2c[t], r3c, T - 1).astype(bf16)
    d4 = [remote(fc_ref.at[c], fc_ref.at[c], p) for p in cpeer]
    for cp in d3g:
        cp.wait_recv()
    fg_ref[c] = total(s2g[t], r3g, T - 1).astype(bf16)
    d4 += [remote(fg_ref.at[c], fg_ref.at[c], p) for p in cpeer]
    for cp in d3b:
        cp.wait_recv()
    fb_ref[c] = total(s2b[t], r3b, T - 1).astype(bf16)
    d4 += [remote(fb_ref.at[c], fb_ref.at[c], p) for p in cpeer]
    for cp in d3v:
        cp.wait_recv()
    fv_ref[...] = vr3[0] + vr3[1] + vr3[2] + vr3[3]
    for cp in d4 + tgc + outc:
        cp.wait_recv()
    oc.wait()
    tc.wait()
    for cp in started:
        cp.wait_send()


def fused_call(geo, lens, x2, og2, pk1, pk2, sm):
    D, C, T, S, L, H, N, U = geo
    R, NS, HD = S * L, N // T, H // D
    f32, bf16 = jnp.float32, jnp.bfloat16
    uq, hs = U // C, NS // 2
    V = pltpu.VMEM
    nsem = 7 + 9 + 9 + 3 + 3 + 6 + 3 + 3 + 4 + 12 + 12 + 9
    any_, vm = pl.BlockSpec(memory_space=pl.ANY), pl.BlockSpec(memory_space=pltpu.VMEM)
    scratch = [
        V((R, H), bf16), V((R, H), bf16), V((R, H), f32), V((R, 128), f32),
        V((R, 2 * N), f32), V((R, 2 * N), f32), V((R, 2 * N), bf16),
        V((R, H), f32), V((R, H), bf16), V((R, H), f32), V((R, H), f32),
        V((R, H), bf16), V((R, H), bf16), V((R, H), bf16), V((R, H), f32), V((R, H), bf16),
        V((R, 2 * N), f32), V((R, 2 * N), bf16), V((R, H), bf16),
        V((4, T, NS, H), bf16), V((T, U, H), bf16), V((D * T, 8, HD), f32),
        V((22, 8, N), f32), V((3, 8, N), f32), V((C - 1, 8, N), f32), V((C - 1, 8, N), f32),
        V((2, T, NS, H), bf16), V((T, U, H), bf16), V((2, T, NS, H), bf16),
        V((2, T, NS, HD), bf16), V((T, U, HD), bf16), V((2, T, NS, HD), bf16),
        V((2, T, NS, HD), bf16), V((T, U, HD), bf16), V((2, T, NS, HD), bf16),
        V((C - 1, T, hs, HD), bf16), V((C - 1, T, uq, HD), bf16), V((C - 1, T, hs, HD), bf16),
        V((T, hs, HD), bf16), V((T, uq, HD), bf16), V((T, hs, HD), bf16),
        V((T - 1, hs, HD), bf16), V((T - 1, uq, HD), bf16), V((T - 1, hs, HD), bf16),
        V((8, H), f32), V((8, H), f32), V((C, 8, H), f32), V((T, 8, H), f32),
        pltpu.SemaphoreType.DMA((4,)), pltpu.SemaphoreType.DMA((nsem,)), pltpu.SemaphoreType.DMA((nsem,)),
    ]
    rows = x2.shape[0]
    return pl.pallas_call(
        functools.partial(fused_body, geo),
        out_shape=(
            jax.ShapeDtypeStruct((rows, U), bf16), jax.ShapeDtypeStruct((rows, U), bf16),
            jax.ShapeDtypeStruct((C, hs, HD), bf16), jax.ShapeDtypeStruct((C, uq, HD), bf16),
            jax.ShapeDtypeStruct((C, hs, HD), bf16), jax.ShapeDtypeStruct((8, H), f32)),
        in_specs=[pl.BlockSpec(memory_space=pltpu.SMEM), any_, any_, vm, vm, vm],
        out_specs=(any_, any_, vm, vm, vm, vm),
        scratch_shapes=scratch,
        compiler_params=pltpu.CompilerParams(
            collective_id=0, has_side_effects=True, vmem_limit_bytes=58 * 1024 * 1024),
        name="block",
    )(lens, x2, og2, pk1, pk2, sm)


def coefficients(lam_re, lam_im, step_log):
    step = jnp.exp(step_log)
    magnitude = jnp.exp(lam_re * step)
    decay_re = magnitude * jnp.cos(lam_im * step)
    decay_im = magnitude * jnp.sin(lam_im * step)
    denom = lam_re * lam_re + lam_im * lam_im
    coef_re = ((decay_re - 1.0) * lam_re + decay_im * lam_im) / denom
    coef_im = (decay_im * lam_re - (decay_re - 1.0) * lam_im) / denom
    return decay_re, decay_im, coef_re, coef_im


def token_split(sizes, inputs, lengths, norm_gain, skip_weight, lambda_re, lambda_im, log_step,
                b_re, b_im, c_re, c_im, glu_weight, glu_bias, out_grad):
    D, C, T = sizes
    seqs, L, H = inputs.shape
    NS, HD = b_re.shape
    U = glu_weight.shape[1]
    geo = (D, C, T, seqs // T, L, H, NS * T, U)
    d, c, t = lax.axis_index("dp"), lax.axis_index("ctx"), lax.axis_index("tp")
    derived, pull = jax.vjp(coefficients, lambda_re, lambda_im, log_step)
    wide = lambda v: jnp.pad(v, (0, HD - v.shape[0]))
    sm = jnp.stack([wide(v) for v in derived + (glu_bias, norm_gain, skip_weight)] + [jnp.zeros((HD,), jnp.float32)])
    pk1 = jnp.stack([b_re, b_im, c_re.T, -c_im.T])
    pk2 = glu_weight.T
    out, tok, fc, fg, fb, fv = fused_call(
        geo, lengths, inputs.reshape(seqs * L, H), out_grad.reshape(seqs * L, U), pk1, pk2, sm)
    pos = c * L + jnp.arange(L, dtype=jnp.int32)
    valid = (pos[None, :] < lengths[:, None])[:, :, None]
    input_grad = jnp.where(valid, out_grad.astype(jnp.float32), 0.0) + tok.reshape(seqs, L, U).astype(jnp.float32)
    place = t * D + d
    own = lambda row, n: lax.dynamic_slice_in_dim(fv[row], place * n, n)
    gl_re, gl_im, g_step = pull(tuple(own(3 + k, NS // D) for k in range(4)))
    gain_g = lax.dynamic_slice_in_dim(fv[0], d * HD, HD)
    skip_g = lax.dynamic_slice_in_dim(fv[1], d * HD, HD)
    up = lambda v: v.astype(jnp.float32)
    fc, fb = up(fc).reshape(2, NS, HD), up(fb).reshape(2, NS, HD)
    return (out.reshape(seqs, L, U), input_grad, gain_g, skip_g, gl_re, gl_im, g_step,
            fb[0], fb[1], fc[0].T, -fc[1].T, up(fg).reshape(U, HD).T, own(2, U // D))


def solution(mesh):
    in_specs = (
        P("dp", "ctx", None),
        P("dp"),
        P("dp"),
        P("dp"),
        P(("tp", "dp")),
        P(("tp", "dp")),
        P(("tp", "dp")),
        P("tp", "dp"),
        P("tp", "dp"),
        P("dp", "tp"),
        P("dp", "tp"),
        P("dp", "tp"),
        P(("tp", "dp")),
        P("dp", "ctx", "tp"),
    )
    out_specs = (
        P("dp", "ctx", "tp"),
        P("dp", "ctx", "tp"),
        P("dp"),
        P("dp"),
        P(("tp", "dp")),
        P(("tp", "dp")),
        P(("tp", "dp")),
        P("tp", "dp"),
        P("tp", "dp"),
        P("dp", "tp"),
        P("dp", "tp"),
        P("dp", "tp"),
        P(("tp", "dp")),
    )
    sizes = tuple(mesh.shape[name] for name in ("dp", "ctx", "tp"))

    def block(*args):
        seqs, _, feat = args[0].shape
        units = args[11].shape[1]
        if sizes == (2, 4, 4) and seqs % sizes[2] == 0 and units % 128 == 0:
            return token_split(sizes, *args)
        return on_device(*args)

    return jax.shard_map(
        block, mesh=mesh, in_specs=in_specs, out_specs=out_specs, check_vma=False
    )
```

profile of v0, /device:TPU:0, one launch (start us, length us, event | category | flops | bytes accessed | tf_op | source)
XLA Modules:
  0.0 103.0 jit_solution(9619858212919083951)
XLA Ops:
  0.6 0.8 negate_bitcast_fusion
  1.4 1.5 %pad_maximum_fusion.refs_3_ = bf16[4,96,256]{2,1,0:T(8,128)(2,1)} fusion(bf16[1,96,256]{2,1,0:T(8,128)(2,1)S(1)} %negate_bitcast_fusion, bf16[1,96,256]{2,1,0:T(8,128)(2,1)} %bitcast.78, bf16[1,96,256]{2,1,0:T(8,128)(2,1)} %bitcast.79, bf16[1,96,256]{2,1,0:T(8,128)(2,1)} %bitcast.80), kind=kLoop, calls=%fused_computation.1 | loop fusion | flops 294912 | bytes 393216 | tf_op jit(solution)/shard_map/stack | solution.py:879
  3.0 1.6 %copy.27 = bf16[256,128]{0,1:T(8,128)(2,1)} copy(bf16[256,128]{1,0:T(8,128)(2,1)} %param.25) | data formatting | bytes 131072 | tf_op args[11]
  4.6 0.7 fusion.21
  5.3 0.7 fusion.22
  6.1 0.7 pad.21
  6.8 1.3 %stack.51.refs_5_ = f32[8,256]{1,0:T(8,128)} concatenate(f32[1,256]{1,0:T(1,128)S(1)} %bitcast.81, f32[1,256]{1,0:T(1,128)S(1)} %bitcast.82, f32[1,256]{1,0:T(1,128)S(1)} %bitcast.83, f32[1,256]{1,0:T(1,128)S(1)} %bitcast.84, f32[1,256]{1,0:T(1,128)S(1)} %bitcast.85, f32[1,256]{1,0:T(1,128)} %bitcast.86, f32[1,256]{1,0:T(1,128)} %bitcast.87, f32[1,256]{1,0:T(1,128)S(1)} %stack_broadcast_in_dim.3), dimensions={0} | concatenate | bytes 16384 | tf_op jit(solution)/shard_map/stack | solution.py:878
  8.1 85.6 %block.1 = (bf16[3072,128]{1,0:T(8,128)(2,1)}, bf16[3072,128]{1,0:T(8,128)(2,1)}, bf16[4,48,256]{2,1,0:T(8,128)(2,1)}, bf16[4,32,256]{2,1,0:T(8,128)(2,1)}, bf16...) custom-call(s32[12]{0:T(128)} %refs_0_.1, bf16[3072,512]{1,0:T(8,128)(2,1)} %bitcast.68, bf16[3072,128]{1,0:T(8,128)(2,1)} %bitcast.69, ...), custom_call_target="tpu_custom_call" | custom-call | tf_op jit(solution)/shard_map/block/pallas_call | solution.py:842
  93.7 0.0 copy-done.9
  93.7 0.1 broadcast_compare_fusion
  93.8 0.0 copy-done
  93.8 0.0 copy-start.5
  93.8 0.0 copy-start.6
  93.8 0.0 copy-start.7
  93.8 0.0 copy-start.2
  93.8 0.0 copy-start.3
  93.8 0.0 copy-start.4
  93.8 2.5 %convert_add_fusion = f32[12,256,128]{2,1,0:T(8,128)} fusion(bf16[12,256,128]{2,1,0:T(8,128)(2,1)} %bitcast.71, bf16[12,256,128]{2,1,0:T(8,128)(2,1)S(1)} %copy-done, pred[12,256]{1,0:T(8,128)(4,1)S(1)} %broadcast_compare_fusion), kind=kLoop, calls=%fused_computation | loop fusion | flops 1572864 | bytes 3148800 | tf_op jit(solution)/shard_map/add | solution.py:885
  96.4 0.0 copy-done.8
  96.4 0.6 constant_dynamic-slice_fusion.5
  97.0 0.0 copy-done.5
  97.0 0.0 copy-done.6
  97.0 0.6 fusion.12
  97.6 0.6 fusion.2
  98.2 0.6 fusion
  98.7 0.0 copy-done.2
  98.7 0.7 fusion.23
  99.4 0.6 slice.50
  100.1 0.6 slice_negate_fusion
  100.8 0.8 copy.28
  101.5 0.6 fusion.11
  102.1 0.9 copy.30
  (17 shorter events, 0.1 us)
Async XLA Ops:
  8.1 85.6 %copy-start.9 = (s32[12]{0:T(128)S(1)}, s32[12]{0:T(128)}, u32[]{:S(2)}) copy-start(s32[12]{0:T(128)} %refs_0_.1) | copy-start | bytes 148
  8.1 85.7 %copy-start = (bf16[12,256,128]{2,1,0:T(8,128)(2,1)S(1)}, bf16[12,256,128]{2,1,0:T(8,128)(2,1)}, u32[]{:S(2)}) copy-start(bf16[12,256,128]{2,1,0:T(8,128)(2,1)} %param.27) | copy-start | bytes 2359300
  93.8 2.6 %copy-start.8 = (f32[8,512]{1,0:T(8,128)S(1)}, f32[8,512]{1,0:T(8,128)}, u32[]{:S(2)}) copy-start(f32[8,512]{1,0:T(8,128)} %get-tuple-element.21) | copy-start | bytes 49156
  93.8 3.2 %copy-start.5 = (f32[48]{0:T(128)S(1)}, f32[48]{0:T(128)}, u32[]{:S(2)}) copy-start(f32[48]{0:T(128)} %param.19) | copy-start | bytes 580
  93.8 3.2 %copy-start.6 = (f32[48]{0:T(128)S(1)}, f32[48]{0:T(128)}, u32[]{:S(2)}) copy-start(f32[48]{0:T(128)} %param.18) | copy-start | bytes 580
  93.8 3.2 %copy-start.7 = (f32[48]{0:T(128)S(1)}, f32[48]{0:T(128)}, u32[]{:S(2)}) copy-start(f32[48]{0:T(128)} %param.20) | copy-start | bytes 580
  93.8 4.9 %copy-start.2 = (bf16[4,48,256]{2,1,0:T(8,128)(2,1)S(1)}, bf16[4,48,256]{2,1,0:T(8,128)(2,1)}, u32[]{:S(2)}) copy-start(bf16[4,48,256]{2,1,0:T(8,128)(2,1)} %get-tuple-element.22) | copy-start | bytes 294916
  93.8 5.6 %copy-start.3 = (bf16[4,48,256]{2,1,0:T(8,128)(2,1)S(1)}, bf16[4,48,256]{2,1,0:T(8,128)(2,1)}, u32[]{:S(2)}) copy-start(bf16[4,48,256]{2,1,0:T(8,128)(2,1)} %get-tuple-element.23) | copy-start | bytes 294916
  93.8 6.9 %copy-start.4 = (bf16[4,32,256]{2,1,0:T(8,128)(2,1)S(1)}, bf16[4,32,256]{2,1,0:T(8,128)(2,1)}, u32[]{:S(2)}) copy-start(bf16[4,32,256]{2,1,0:T(8,128)(2,1)} %get-tuple-element.24) | copy-start | bytes 196612
  96.4 5.8 %copy-start.1 = (bf16[3072,128]{1,0:T(8,128)(2,1)S(1)}, bf16[3072,128]{1,0:T(8,128)(2,1)}, u32[]{:S(2)}) copy-start(bf16[3072,128]{1,0:T(8,128)(2,1)} %get-tuple-element.19) | copy-start | bytes 2359300
where the time goes:
time: 103 us
  Pallas kernels  85.6 us (83%)
  other arithmetic  8.89 us (9%)
  local copies, waits for them, and re-layouts  7.74 us (8%)
    pallas_call x1, Pallas kernels, fused_call(): pl.pallas_call(functools.partial(fused_body, geo), out_shape=(jax.ShapeDt...  85.6 us
    add x1, other arithmetic, token_split(): jnp.where(valid, out_grad.astype(jnp.float32), 0.0)  2.53 us
    unnamed x22, local copies, waits for them, and re-layouts  2.5 us
    another operation x2, other arithmetic, token_split(): pk1 = jnp.stack([b_re, b_im, c_re.T, -c_im.T])  2.35 us

commit v1 on v0

--- a/solution.py
+++ b/solution.py
@@ -325,10 +325,11 @@
     NS = N // T
     HD = H // D
     f32, bf16 = jnp.float32, jnp.bfloat16
-    (len_ref, x_hbm, og_hbm, pk1, pk2, sm_ref, out_hbm, tg_hbm, fc_ref, fg_ref, fb_ref, fv_ref) = refs[:12]
+    (len_ref, x_hbm, og_hbm, bre, bim, cre, cim, glu, gain_in, skip_in, lre_in, lim_in, stp_in, bias_in,
+     out_hbm, tg_hbm, fc_ref, fg_ref, fb_ref, fv_ref) = refs[:20]
     (xv, nrm, xh, rs, raw, st, sb, tmp, act, gp, sig, ogv, ob, gl, pg, plb, mu, nb, tgb,
      w4, gt, smr, cst, ce, cer, cbr, gc, gg, gb, r1c, r1g, r1b, s1c, s1g, s1b, r2c, r2g, r2b,
-     s2c, s2g, s2b, r3c, r3g, r3b, vv, vr1, vr2, vr3, lsem, ssem, rsem) = refs[12:]
+     s2c, s2g, s2b, r3c, r3g, r3b, vv, vr1, vr2, vr3, vf, pk, sm_ref, lsem, ssem, rsem) = refs[20:]
     d, c, t = lax.axis_index("dp"), lax.axis_index("ctx"), lax.axis_index("tp")
     zpeer = [(d, c, lax.rem(t + k, T)) for k in range(1, T)]
     cpeer = [(d, lax.rem(c + k, C), t) for k in range(1, C)]
@@ -357,35 +358,47 @@
     barrier = pltpu.get_barrier_semaphore()
     for p in everyone:
         pl.semaphore_signal(barrier, inc=1, device_id=p, device_id_type=MESH)
+    pk[0], pk[1], pk[2], pk[3] = bre[...], bim[...], cre[...], cim[...]
+    sm_ref[...] = jnp.zeros_like(sm_ref)
+    own = coefficients(lre_in[...], lim_in[...], stp_in[...])
+    for k in range(4):
+        sm_ref[k:k + 1, 0:NS // D] = own[k]
+    sm_ref[4:5, 0:U // D] = bias_in[...]
+    sm_ref[5:6, :] = gain_in[...]
+    sm_ref[6:7, :] = skip_in[...]
     pl.semaphore_wait(barrier, len(everyone))
 
     me8 = d * T + t
     small = [remote(sm_ref, smr.at[me8], p) for p in zpeer + [sib] + xpeer]
     gq, hq = c // 2, lax.rem(c, 2)
     wl = lane(HD * d + 128 * hq, 128)
-    w1b = [remote(pk1.at[gq, :, lane(128 * hq, 128)], w4.at[gq, t, :, wl], p) for p in zpeer]
-    w1c = [remote(pk1.at[2 + gq, :, lane(128 * hq, 128)], w4.at[2 + gq, t, :, wl], p) for p in zpeer]
-    uq = U // C
-    grow = pl.ds(pl.multiple_of(uq * c, uq), uq)
+    w1b = [remote(pk.at[gq, :, lane(128 * hq, 128)], w4.at[gq, t, :, wl], p) for p in zpeer]
+    w1c = [remote(pk.at[2 + gq, :, lane(128 * hq, 128)], w4.at[2 + gq, t, :, wl], p) for p in zpeer]
+    uq = HD // C
+    gown = pl.ds(pl.multiple_of(uq * c, uq), uq)
+    grow = pl.ds(pl.multiple_of(HD * d + uq * c, uq), uq)
+    dr_ = pl.ds(pl.multiple_of(HD * d, HD), HD)
     dl = lane(HD * d, HD)
-    w1g = [remote(pk2.at[grow], gt.at[t, grow, dl], p) for p in zpeer]
-    w4[gq, t, :, wl] = pk1[gq, :, lane(128 * hq, 128)]
-    w4[2 + gq, t, :, wl] = pk1[2 + gq, :, lane(128 * hq, 128)]
-    gt[t, grow, dl] = pk2[grow]
+    tl = lane(U * t, U)
+    w1g = [remote(glu.at[gown], gt.at[grow, tl], p) for p in zpeer]
+    w4[gq, t, :, wl] = pk[gq, :, lane(128 * hq, 128)]
+    w4[2 + gq, t, :, wl] = pk[2 + gq, :, lane(128 * hq, 128)]
+    gt[grow, tl] = glu[gown]
     smr[me8] = sm_ref[...]
 
     cx.wait()
 
     def ln_tile(i, _):
-        rows = pl.ds(pl.multiple_of(i * 32, 32), 32)
-        x = xv[rows, :].astype(f32)
-        cen = x - jnp.mean(x, -1, keepdims=True)
-        rstd = lax.rsqrt(jnp.mean(cen * cen, -1, keepdims=True) + epsilon)
-        xh[rows, :] = cen * rstd
-        rs[rows, :] = jnp.broadcast_to(rstd, (32, 128))
-        return 0
-
-    lax.fori_loop(0, R // 32, ln_tile, 0)
+        for u in range(4):
+            rows = pl.ds(pl.multiple_of(i * 128 + u * 32, 32), 32)
+            x = xv[rows, :].astype(f32)
+            cen = x - jnp.mean(x, -1, keepdims=True)
+            rstd = lax.rsqrt(jnp.mean(cen * cen, -1, keepdims=True) + epsilon)
+            xh[rows, :] = cen * rstd
+            rs[rows, :] = jnp.broadcast_to(rstd, (32, 128))
+        return 0
+
+    lax.fori_loop(0, R // 128, ln_tile, 0)
 
     for cp in small:
         cp.wait_recv()
@@ -440,14 +453,14 @@
     for cp in w1b:
         cp.wait_recv()
     w2b = [remote(w4.at[gq, :, :, wl], w4.at[gq, :, :, wl], p) for p in cpeer]
+    og = [remote(og_hbm.at[pl.ds(pl.multiple_of(R * p[2], R), R)], ogv.at[:, lane(U * t, U)], p)
+          for p in zpeer]
     for cp in w1c:
         cp.wait_recv()
     w2c = [remote(w4.at[2 + gq, :, :, wl], w4.at[2 + gq, :, :, wl], p) for p in cpeer]
     for cp in w1g:
         cp.wait_recv()
-    w2g = [remote(gt.at[:, grow, dl], gt.at[:, grow, dl], p) for p in cpeer]
-    og = [remote(og_hbm.at[pl.ds(pl.multiple_of(R * p[2], R), R)], ogv.at[:, lane(U * t, U)], p)
-          for p in zpeer]
+    w2g = [remote(gt.at[grow, :], gt.at[grow, :], p) for p in cpeer]
     for cp in w2b:
         cp.wait_recv()
     w3b = remote(w4.at[0:2, :, :, dl], w4.at[0:2, :, :, dl], sib)
@@ -456,7 +469,7 @@
     w3c = remote(w4.at[2:4, :, :, dl], w4.at[2:4, :, :, dl], sib)
     for cp in w2g:
         cp.wait_recv()
-    w3g = remote(gt.at[:, :, dl], gt.at[:, :, dl], sib)
+    w3g = remote(gt.at[dr_, :], gt.at[dr_, :], sib)
 
     w3b.wait_recv()
 
@@ -475,30 +488,41 @@
             con = [cst[base + k, :, lr_] for k in range(8)]
             cfr, cfi = cst[18, :, lr_], cst[19, :, lr_]
 
+            e = 0 if reverse else 7
+            e0 = cst[16, :, lr_]
+            e1 = -cst[17, :, lr_] if reverse else cst[17, :, lr_]
+
             def tile(i, carry):
-                ii = L // 8 - 1 - i if reverse else i
-                out = []
+                carry = list(carry)
+                ii = L // 32 - 1 - i if reverse else i
                 for s in range(S):
-                    rows = pl.ds(pl.multiple_of(s * L + ii * 8, 8), 8)
-                    ar, ai = src[rows, lr_], src[rows, li_]
-                    if coef:
-                        ar, ai = cmul(cfr, cfi, ar, ai)
-                    for n_, k in ((0, 1), (1, 2), (2, 4)):
-                        sh = 8 - k if reverse else k
-                        br, bi = pltpu.roll(ar, sh, 0), pltpu.roll(ai, sh, 0)
-                        mr, mi = con[2 * n_], con[2 * n_ + 1]
-                        ar, ai = ar + mr * br - mi * bi, ai + mr * bi + mi * br
+                    loc = []
+                    for u in range(4):
+                        uu = 3 - u if reverse else u
+                        rows = pl.ds(pl.multiple_of(s * L + ii * 32 + uu * 8, 8), 8)
+                        ar, ai = src[rows, lr_], src[rows, li_]
+                        if coef:
+                            ar, ai = cmul(cfr, cfi, ar, ai)
+                        else:
+                            ai = -ai
+                        for n_, k in ((0, 1), (1, 2), (2, 4)):
+                            sh = 8 - k if reverse else k
+                            br, bi = pltpu.roll(ar, sh, 0), pltpu.roll(ai, sh, 0)
+                            mr, mi = con[2 * n_], con[2 * n_ + 1]
+                            ar, ai = ar + mr * br - mi * bi, ai + mr * bi + mi * br
+                        loc.append((rows, ar, ai))
                     kr, ki = carry[2 * s], carry[2 * s + 1]
-                    ar, ai = ar + con[6] * kr - con[7] * ki, ai + con[6] * ki + con[7] * kr
-                    dst[rows, lr_] = ar
-                    dst[rows, li_] = ai
-                    e = 0 if reverse else 7
-                    out.append(jnp.broadcast_to(ar[e:e + 1, :], (8, 128)))
-                    out.append(jnp.broadcast_to(ai[e:e + 1, :], (8, 128)))
-                return tuple(out)
+                    for rows, ar, ai in loc:
+                        dst[rows, lr_] = ar + con[6] * kr - con[7] * ki
+                        dst[rows, li_] = ai + con[6] * ki + con[7] * kr
+                        endr = jnp.broadcast_to(ar[e:e + 1, :], (8, 128))
+                        endi = jnp.broadcast_to(ai[e:e + 1, :], (8, 128))
+                        kr, ki = endr + e0 * kr - e1 * ki, endi + e0 * ki + e1 * kr
+                    carry[2 * s], carry[2 * s + 1] = kr, ki
+                return tuple(carry)
 
             z = jnp.zeros((8, 128), f32)
-            fin = lax.fori_loop(0, L // 8, tile, (z,) * (2 * S))
+            fin = lax.fori_loop(0, L // 32, tile, (z,) * (2 * S))
             for s in range(S):
                 end_ref[pl.ds(s, 1), lr_] = fin[2 * s][0:1, :]
                 end_ref[pl.ds(S + s, 1), lr_] = fin[2 * s + 1][0:1, :]
@@ -554,7 +578,7 @@
                     q[2 * s], q[2 * s + 1] = cmul(q[2 * s], q[2 * s + 1], e0, e1)
                 rows = pl.ds(pl.multiple_of(s * L + i * 16, 16), 16)
                 sb[rows, lr_] = jnp.concatenate(rr, 0).astype(bf16)
-                sb[rows, li_] = jnp.concatenate(ri, 0).astype(bf16)
+                sb[rows, li_] = (-jnp.concatenate(ri, 0)).astype(bf16)
             return tuple(q)
 
         lax.fori_loop(0, L // 16, tile, q0)
@@ -584,7 +608,7 @@
     w3g.wait_recv()
 
     def gate_seq(s, _):
-        tmp[seq_rows(s), :] = nt(act[seq_rows(s), :], gt[...].reshape(H, H))
+        tmp[seq_rows(s), :] = nn(act[seq_rows(s), :], gt[...])
         return 0
 
     lax.fori_loop(0, S, gate_seq, 0)
@@ -627,7 +651,7 @@
     bias_g = lax.fori_loop(0, R // 32, gate_tile, jnp.zeros((8, H), f32))
 
     def actg_seq(s, _):
-        tmp[seq_rows(s), :] = nn(gl[seq_rows(s), :], gt[...].reshape(H, H))
+        tmp[seq_rows(s), :] = nt(gl[seq_rows(s), :], gt[...])
         return 0
 
     lax.fori_loop(0, S, actg_seq, 0)
@@ -649,22 +673,22 @@
     scan_lanes(mu, mu, 8, False, True, ce.at[1])
     bce = [remote(ce.at[1], cbr.at[k], p) for k, p in enumerate(cpeer)]
 
-    gcf, gbf, ggf = gc.reshape(2 * N, H), gb.reshape(2 * N, H), gg.reshape(H, H)
+    gcf, gbf = gc.reshape(2 * N, H), gb.reshape(2 * N, H)
 
     def gc_step(j, _):
-        gcf[pl.ds(pl.multiple_of(j * 128, 128), 128), :] = tn(sb[:, lane(j * 128, 128)], plb[...]).astype(bf16)
-        return 0
-
-    lax.fori_loop(0, 2 * N // 128, gc_step, 0)
+        gcf[pl.ds(pl.multiple_of(j * 256, 256), 256), :] = tn(sb[:, lane(j * 256, 256)], plb[...]).astype(bf16)
+        return 0
+
+    lax.fori_loop(0, 2 * N // 256, gc_step, 0)
     ol = lane(HD * (1 - d), HD)
     d1c = remote(gc.at[:, :, :, ol], r1c, sib)
 
     def gg_step(j, _):
-        ggf[pl.ds(pl.multiple_of(j * 128, 128), 128), :] = tn(gl[:, lane(j * 128, 128)], act[...]).astype(bf16)
-        return 0
-
-    lax.fori_loop(0, H // 128, gg_step, 0)
-    d1g = remote(gg.at[:, :, ol], r1g, sib)
+        gg[pl.ds(pl.multiple_of(j * 256, 256), 256), :] = tn(act[:, lane(j * 256, 256)], gl[...]).astype(bf16)
+        return 0
+
+    lax.fori_loop(0, H // 256, gg_step, 0)
+    d1g = remote(gg.at[pl.ds(pl.multiple_of(HD * (1 - d), HD), HD), :], r1g, sib)
 
     for cp in bce:
         cp.wait_recv()
@@ -718,10 +742,10 @@
     lax.fori_loop(0, N // 128, adj_lanes, 0)
 
     def gb_step(j, _):
-        gbf[pl.ds(pl.multiple_of(j * 128, 128), 128), :] = tn(nb[:, lane(j * 128, 128)], nrm[...]).astype(bf16)
-        return 0
-
-    lax.fori_loop(0, 2 * N // 128, gb_step, 0)
+        gbf[pl.ds(pl.multiple_of(j * 256, 256), 256), :] = tn(nb[:, lane(j * 256, 256)], nrm[...]).astype(bf16)
+        return 0
+
+    lax.fori_loop(0, 2 * N // 256, gb_step, 0)
     d1b = remote(gb.at[:, :, :, ol], r1b, sib)
 
     def rs_ctx(p):
@@ -731,9 +755,9 @@
     s1c[...] = (gc[:, :, :, dl].astype(f32) + r1c[...].astype(f32)).astype(bf16)
     d2c = [remote(s1c.at[rs_ctx(p[1])[0], :, rs_ctx(p[1])[1], :], r2c.at[k], p) for k, p in enumerate(cpeer)]
     d1g.wait_recv()
-    s1g[...] = (gg[:, :, dl].astype(f32) + r1g[...].astype(f32)).astype(bf16)
+    s1g[...] = (gg[dr_, :].astype(f32) + r1g[...].astype(f32)).astype(bf16)
     gr = lambda p: pl.ds(pl.multiple_of(uq * p, uq), uq)
-    d2g = [remote(s1g.at[:, gr(p[1]), :], r2g.at[k], p) for k, p in enumerate(cpeer)]
+    d2g = [remote(s1g.at[gr(p[1]), :], r2g.at[k], p) for k, p in enumerate(cpeer)]
 
     def ng_seq(s, _):
         tmp[seq_rows(s), :] = nn(nb[seq_rows(s), :], w4[0:2].reshape(2 * N, H))
@@ -742,16 +766,18 @@
     lax.fori_loop(0, S, ng_seq, 0)
 
     def tok_tile(i, acc):
-        rows = pl.ds(pl.multiple_of(i * 32, 32), 32)
-        n = tmp[rows, :] + skip_r * pg[rows, :]
-        xt = xh[rows, :]
-        h = n * gain_r
-        m1 = jnp.mean(h, -1, keepdims=True)
-        m2 = jnp.mean(h * xt, -1, keepdims=True)
-        tgb[rows, :] = ((h - m1 - xt * m2) * rs[rows, 0:1]).astype(bf16)
-        return acc + fold(n * xt)
-
-    gain_g = lax.fori_loop(0, R // 32, tok_tile, jnp.zeros((8, H), f32))
+        for u in range(4):
+            rows = pl.ds(pl.multiple_of(i * 128 + u * 32, 32), 32)
+            n = tmp[rows, :] + skip_r * pg[rows, :]
+            xt = xh[rows, :]
+            h = n * gain_r
+            m1 = jnp.mean(h, -1, keepdims=True)
+            m2 = jnp.mean(h * xt, -1, keepdims=True)
+            tgb[rows, :] = ((h - m1 - xt * m2) * rs[rows, 0:1]).astype(bf16)
+            acc = acc + fold(n * xt)
+        return acc
+
+    gain_g = lax.fori_loop(0, R // 128, tok_tile, jnp.zeros((8, H), f32))
     tgc = [remote(tgb.at[:, lane(U * p[2], U)], tg_hbm.at[mine, :], p) for p in zpeer]
     tc = pltpu.make_async_copy(tgb.at[:, lane(U * t, U)], tg_hbm.at[mine, :], lsem.at[3])
     tc.start()
@@ -779,8 +805,8 @@
     d3c = [remote(s2c.at[p[2]], r3c.at[k], p) for k, p in enumerate(zpeer)]
     for cp in d2g:
         cp.wait_recv()
-    s2g[...] = total(s1g[:, gr(c), :], r2g, C - 1).astype(bf16)
-    d3g = [remote(s2g.at[p[2]], r3g.at[k], p) for k, p in enumerate(zpeer)]
+    s2g[...] = total(s1g[gr(c), :], r2g, C - 1).astype(bf16)
+    d3g = [remote(s2g.at[:, lane(U * p[2], U)], r3g.at[k], p) for k, p in enumerate(zpeer)]
     for cp in d2b:
         cp.wait_recv()
     s2b[...] = total(s1b[rs_ctx(c)[0], :, rs_ctx(c)[1], :], r2b, C - 1).astype(bf16)
@@ -796,7 +822,7 @@
     d4 = [remote(fc_ref.at[c], fc_ref.at[c], p) for p in cpeer]
     for cp in d3g:
         cp.wait_recv()
-    fg_ref[c] = total(s2g[t], r3g, T - 1).astype(bf16)
+    fg_ref[c] = total(s2g[:, tl], r3g, T - 1).astype(bf16)
     d4 += [remote(fg_ref.at[c], fg_ref.at[c], p) for p in cpeer]
     for cp in d3b:
         cp.wait_recv()
@@ -804,7 +830,27 @@
     d4 += [remote(fb_ref.at[c], fb_ref.at[c], p) for p in cpeer]
     for cp in d3v:
         cp.wait_recv()
-    fv_ref[...] = vr3[0] + vr3[1] + vr3[2] + vr3[3]
+    vf[...] = vr3[0] + vr3[1] + vr3[2] + vr3[3]
+    place = t * D + d
+    back = lambda n: lax.rem(H - n * place, H)
+    st8 = pltpu.roll(vf[...], back(NS // D), 1)[:, 0:NS // D]
+    ub8 = pltpu.roll(vf[...], back(U // D), 1)[:, 0:U // D]
+    lr1, li1, step1 = lre_in[...], lim_in[...], jnp.exp(stp_in[...])
+    dr1, di1, cr1, ci1 = (sm_ref[k:k + 1, 0:NS // D] for k in range(4))
+    gdr, gdi, gcr, gci = (st8[k:k + 1] for k in range(3, 7))
+    inv = 1.0 / (lr1 * lr1 + li1 * li1)
+    hdr = gdr + (gcr * lr1 - gci * li1) * inv
+    hdi = gdi + (gcr * li1 + gci * lr1) * inv
+    pull = 2.0 * (gcr * cr1 + gci * ci1)
+    e1, e2 = dr1 - 1.0, hdr * dr1 + hdi * di1
+    e3 = hdi * dr1 - hdr * di1
+    fv_ref[...] = jnp.zeros_like(fv_ref)
+    fv_ref[0:1, :] = vf[0:1, dl]
+    fv_ref[1:2, :] = vf[1:2, dl]
+    fv_ref[2:3, 0:U // D] = ub8[2:3]
+    fv_ref[3:4, 0:NS // D] = (gcr * e1 + gci * di1 - pull * lr1) * inv + step1 * e2
+    fv_ref[4:5, 0:NS // D] = (gcr * di1 - gci * e1 - pull * li1) * inv + step1 * e3
+    fv_ref[5:6, 0:NS // D] = step1 * (lr1 * e2 + li1 * e3)
     for cp in d4 + tgc + outc:
         cp.wait_recv()
     oc.wait()
@@ -813,11 +859,11 @@
         cp.wait_send()
 
 
-def fused_call(geo, lens, x2, og2, pk1, pk2, sm):
+def fused_call(geo, lens, x2, og2, *params):
     D, C, T, S, L, H, N, U = geo
     R, NS, HD = S * L, N // T, H // D
     f32, bf16 = jnp.float32, jnp.bfloat16
-    uq, hs = U // C, NS // 2
+    uq, hs = HD // C, NS // 2
     V = pltpu.VMEM
     nsem = 7 + 9 + 9 + 3 + 3 + 6 + 3 + 3 + 4 + 12 + 12 + 9
     any_, vm = pl.BlockSpec(memory_space=pl.ANY), pl.BlockSpec(memory_space=pltpu.VMEM)
@@ -827,15 +873,16 @@
         V((R, H), f32), V((R, H), bf16), V((R, H), f32), V((R, H), f32),
         V((R, H), bf16), V((R, H), bf16), V((R, H), bf16), V((R, H), f32), V((R, H), bf16),
         V((R, 2 * N), f32), V((R, 2 * N), bf16), V((R, H), bf16),
-        V((4, T, NS, H), bf16), V((T, U, H), bf16), V((D * T, 8, HD), f32),
+        V((4, T, NS, H), bf16), V((H, H), bf16), V((D * T, 8, HD), f32),
         V((22, 8, N), f32), V((3, 8, N), f32), V((C - 1, 8, N), f32), V((C - 1, 8, N), f32),
-        V((2, T, NS, H), bf16), V((T, U, H), bf16), V((2, T, NS, H), bf16),
-        V((2, T, NS, HD), bf16), V((T, U, HD), bf16), V((2, T, NS, HD), bf16),
-        V((2, T, NS, HD), bf16), V((T, U, HD), bf16), V((2, T, NS, HD), bf16),
-        V((C - 1, T, hs, HD), bf16), V((C - 1, T, uq, HD), bf16), V((C - 1, T, hs, HD), bf16),
-        V((T, hs, HD), bf16), V((T, uq, HD), bf16), V((T, hs, HD), bf16),
-        V((T - 1, hs, HD), bf16), V((T - 1, uq, HD), bf16), V((T - 1, hs, HD), bf16),
-        V((8, H), f32), V((8, H), f32), V((C, 8, H), f32), V((T, 8, H), f32),
+        V((2, T, NS, H), bf16), V((H, H), bf16), V((2, T, NS, H), bf16),
+        V((2, T, NS, HD), bf16), V((HD, H), bf16), V((2, T, NS, HD), bf16),
+        V((2, T, NS, HD), bf16), V((HD, H), bf16), V((2, T, NS, HD), bf16),
+        V((C - 1, T, hs, HD), bf16), V((C - 1, uq, H), bf16), V((C - 1, T, hs, HD), bf16),
+        V((T, hs, HD), bf16), V((uq, H), bf16), V((T, hs, HD), bf16),
+        V((T - 1, hs, HD), bf16), V((T - 1, uq, U), bf16), V((T - 1, hs, HD), bf16),
+        V((8, H), f32), V((8, H), f32), V((C, 8, H), f32), V((T, 8, H), f32), V((8, H), f32),
+        V((4, NS, HD), bf16), V((8, HD), f32),
         pltpu.SemaphoreType.DMA((4,)), pltpu.SemaphoreType.DMA((nsem,)), pltpu.SemaphoreType.DMA((nsem,)),
     ]
     rows = x2.shape[0]
@@ -843,15 +890,65 @@
         functools.partial(fused_body, geo),
         out_shape=(
             jax.ShapeDtypeStruct((rows, U), bf16), jax.ShapeDtypeStruct((rows, U), bf16),
-            jax.ShapeDtypeStruct((C, hs, HD), bf16), jax.ShapeDtypeStruct((C, uq, HD), bf16),
-            jax.ShapeDtypeStruct((C, hs, HD), bf16), jax.ShapeDtypeStruct((8, H), f32)),
-        in_specs=[pl.BlockSpec(memory_space=pltpu.SMEM), any_, any_, vm, vm, vm],
+            jax.ShapeDtypeStruct((C, hs, HD), bf16), jax.ShapeDtypeStruct((C, uq, U), bf16),
+            jax.ShapeDtypeStruct((C, hs, HD), bf16), jax.ShapeDtypeStruct((8, HD), f32)),
+        in_specs=[pl.BlockSpec(memory_space=pltpu.SMEM), any_, any_] + [vm] * 11,
         out_specs=(any_, any_, vm, vm, vm, vm),
         scratch_shapes=scratch,
         compiler_params=pltpu.CompilerParams(
             collective_id=0, has_side_effects=True, vmem_limit_bytes=58 * 1024 * 1024),
         name="block",
-    )(lens, x2, og2, pk1, pk2, sm)
+    )(lens, x2, og2, *params)
+
+
+def finish_body(geo, group, len_ref, out_in, tok_in, og_in, fc, fg, fb, fv, out, ingrad, gain_g, skip_g,
+                lre_g, lim_g, step_g, bre_g, bim_g, cre_g, cim_g, glu_g, bias_g):
+    D, C, T, S, L, H, N, U = geo
+    NS = N // T
+    f32 = jnp.float32
+    i = pl.program_id(0)
+    out[...] = out_in[...]
+    pos = lax.axis_index("ctx") * L + lax.broadcasted_iota(jnp.int32, (L, 1), 0)
+    for s in range(group):
+        keep = jnp.where(pos < len_ref[i * group + s], 1.0, 0.0)
+        ingrad[s] = keep * og_in[s].astype(f32) + tok_in[s].astype(f32)
+
+    @pl.when(i == 0)
+    def _():
+        h = C // 2
+        for k in range(C):
+            rows = pl.ds((k % h) * (NS // h), NS // h)
+            (bre_g if k < h else bim_g)[rows, :] = fb[k].astype(f32)
+            (cre_g if k < h else cim_g)[rows, :] = fc[k].astype(f32)
+        glu_g[...] = fg[...].reshape(glu_g.shape).astype(f32)
+        gain_g[...] = fv[0:1, :]
+        skip_g[...] = fv[1:2, :]
+        bias_g[...] = fv[2:3, 0:U // D]
+        lre_g[...] = fv[3:4, 0:NS // D]
+        lim_g[...] = fv[4:5, 0:NS // D]
+        step_g[...] = fv[5:6, 0:NS // D]
+
+
+def finish_call(geo, lens, out, tok, og, fc, fg, fb, fv):
+    D, C, T, S, L, H, N, U = geo
+    NS, HD = N // T, H // D
+    f32 = jnp.float32
+    seqs = S * T
+    group = 2
+    big = pl.BlockSpec((group, L, U), lambda i: (i, 0, 0))
+    vm = pl.BlockSpec(memory_space=pltpu.VMEM)
+    const = lambda *shape: pl.BlockSpec(shape, lambda i: (0,) * len(shape))
+    small = [(1, HD), (1, HD)] + [(1, NS // D)] * 3 + [(NS, HD)] * 4 + [(HD, U), (1, U // D)]
+    return pl.pallas_call(
+        functools.partial(finish_body, geo, group),
+        grid=(seqs // group,),
+        out_shape=[jax.ShapeDtypeStruct((seqs, L, U), jnp.bfloat16), jax.ShapeDtypeStruct((seqs, L, U), f32)]
+        + [jax.ShapeDtypeStruct(s, f32) for s in small],
+        in_specs=[pl.BlockSpec(memory_space=pltpu.SMEM), big, big, big] + [const(*a.shape) for a in (fc, fg, fb, fv)],
+        out_specs=[big, big] + [const(*s) for s in small],
+        compiler_params=pltpu.CompilerParams(vmem_limit_bytes=60 * 1024 * 1024),
+        name="finish",
+    )(lens, out.reshape(seqs, L, U), tok.reshape(seqs, L, U), og, fc, fg, fb, fv)
 
 
 def coefficients(lam_re, lam_im, step_log):
@@ -859,9 +956,9 @@
     magnitude = jnp.exp(lam_re * step)
     decay_re = magnitude * jnp.cos(lam_im * step)
     decay_im = magnitude * jnp.sin(lam_im * step)
-    denom = lam_re * lam_re + lam_im * lam_im
-    coef_re = ((decay_re - 1.0) * lam_re + decay_im * lam_im) / denom
-    coef_im = (decay_im * lam_re - (decay_re - 1.0) * lam_im) / denom
+    inv = 1.0 / (lam_re * lam_re + lam_im * lam_im)
+    coef_re = ((decay_re - 1.0) * lam_re + decay_im * lam_im) * inv
+    coef_im = (decay_im * lam_re - (decay_re - 1.0) * lam_im) * inv
     return decay_re, decay_im, coef_re, coef_im
 
 
@@ -872,26 +969,16 @@
     NS, HD = b_re.shape
     U = glu_weight.shape[1]
     geo = (D, C, T, seqs // T, L, H, NS * T, U)
-    d, c, t = lax.axis_index("dp"), lax.axis_index("ctx"), lax.axis_index("tp")
-    derived, pull = jax.vjp(coefficients, lambda_re, lambda_im, log_step)
-    wide = lambda v: jnp.pad(v, (0, HD - v.shape[0]))
-    sm = jnp.stack([wide(v) for v in derived + (glu_bias, norm_gain, skip_weight)] + [jnp.zeros((HD,), jnp.float32)])
-    pk1 = jnp.stack([b_re, b_im, c_re.T, -c_im.T])
-    pk2 = glu_weight.T
+    row = lambda v: v.reshape(1, -1)
     out, tok, fc, fg, fb, fv = fused_call(
-        geo, lengths, inputs.reshape(seqs * L, H), out_grad.reshape(seqs * L, U), pk1, pk2, sm)
-    pos = c * L + jnp.arange(L, dtype=jnp.int32)
-    valid = (pos[None, :] < lengths[:, None])[:, :, None]
-    input_grad = jnp.where(valid, out_grad.astype(jnp.float32), 0.0) + tok.reshape(seqs, L, U).astype(jnp.float32)
-    place = t * D + d
-    own = lambda row, n: lax.dynamic_slice_in_dim(fv[row], place * n, n)
-    gl_re, gl_im, g_step = pull(tuple(own(3 + k, NS // D) for k in range(4)))
-    gain_g = lax.dynamic_slice_in_dim(fv[0], d * HD, HD)
-    skip_g = lax.dynamic_slice_in_dim(fv[1], d * HD, HD)
-    up = lambda v: v.astype(jnp.float32)
-    fc, fb = up(fc).reshape(2, NS, HD), up(fb).reshape(2, NS, HD)
-    return (out.reshape(seqs, L, U), input_grad, gain_g, skip_g, gl_re, gl_im, g_step,
-            fb[0], fb[1], fc[0].T, -fc[1].T, up(fg).reshape(U, HD).T, own(2, U // D))
+        geo, lengths, inputs.reshape(seqs * L, H), out_grad.reshape(seqs * L, U),
+        b_re, b_im, c_re.T, c_im.T, glu_weight,
+        *(row(v) for v in (norm_gain, skip_weight, lambda_re, lambda_im, log_step, glu_bias)))
+    res = finish_call(geo, lengths, out, tok, out_grad, fc, fg, fb, fv)
+    out, ingrad, gain_g, skip_g, lre_g, lim_g, step_g, bre_g, bim_g, cre_g, cim_g, glu_g, bias_g = res
+    flat = lambda v: v.reshape(-1)
+    return (out, ingrad, flat(gain_g), flat(skip_g), flat(lre_g), flat(lim_g), flat(step_g),
+            bre_g, bim_g, cre_g.T, cim_g.T, glu_g, flat(bias_g))
 
 
 def solution(mesh):

time: 103 us -> 90.3 us (0.88)
  the two profiles are of different devices: /device:TPU:0 before, /device:TPU:24 now
where the time goes in v1:
time: 90.3 us; the launch traced here: 90 us
  Pallas kernels  89.3 us (99%)
    pallas_call x1, Pallas kernels, fused_call(): pl.pallas_call(functools.partial(fused_body, geo), out_shape=(jax.ShapeDt...  83.7 us
    pallas_call x1, Pallas kernels, finish_call(): pl.pallas_call(functools.partial(finish_body, geo, group), grid=(seqs //...  5.62 us

profile of v1, /device:TPU:24, one launch (start us, length us, event | category | flops | bytes accessed | tf_op | source)
XLA Modules:
  0.0 90.0 jit_solution(3267721643229628977)
XLA Ops:
  0.6 83.7 %block.1 = (bf16[3072,128]{1,0:T(8,128)(2,1)}, bf16[3072,128]{1,0:T(8,128)(2,1)}, bf16[4,48,256]{2,1,0:T(8,128)(2,1)}, bf16[4,64,128]{2,1,0:T(8,128)(2,1)}, bf16...) custom-call(s32[12]{0:T(128)} %len_ref.1, bf16[3072,512]{1,0:T(8,128)(2,1)} %bitcast.20, bf16[3072,128]{1,0:T(8,128)(2,1)} %bitcast.21, ...), custom_call_target="tpu_custom_call" | custom-call | tf_op jit(solution)/shard_map/block/pallas_call | solution.py:889
  84.4 5.6 %finish.1 = (bf16[12,256,128]{2,1,0:T(8,128)(2,1)}, f32[12,256,128]{2,1,0:T(8,128)}, f32[1,256]{1,0:T(1,128)}, f32[1,256]{1,0:T(1,128)}, f32[1,48]{1,0:T(1,128)}...) custom-call(s32[12]{0:T(128)} %len_ref.1, ...), custom_call_target="tpu_custom_call" | custom-call | tf_op jit(solution)/shard_map/finish/pallas_call | solution.py:942
